TPU v7x, 256 devices: a whole 4x4x8 slice. The times are simulated.
256 devices in a mesh: seq: 64 (over z, x, core), head: 4 (over y).
Axes of the slice: x: 4, y: 4, z: 8, core: 2. Of those that a mesh axis runs over, the one named last changes fastest.
Arguments:
- queries: bfloat16 [32768, 4096], P('seq', 'head'), may hold values from -6 to 6
- keys: bfloat16 [32768, 4096], P('seq', 'head'), may hold values from -6 to 6
- values: bfloat16 [32768, 4096], P('seq', 'head'), may hold values from -6 to 6
- level_weights: float32 [32, 9, 32768], P('head', None, 'seq'), may hold values from 0.5 to 1.5
- out_weight: bfloat16 [4096, 4096], P('head'), may hold values from -0.125 to 0.125
Outputs:
- mixed: bfloat16 [32768, 4096], P('seq', 'head')
All inputs are finite; a program needn't handle non-finite values.
Results may differ from a plain program's by a relative error of at most 0.017.
Values may be sent and summed in bfloat16 or wider, within the bound.
A program may use at most 128 MiB of HBM per device.

v0:
```python
import jax
import jax.numpy as jnp
from jax import lax
from jax.sharding import PartitionSpec as P

BLOCK = 128


epsilon = 1e-06


def partner_2(array, axis, apart):
    return lax.ppermute(array, axis, [(i, i ^ 1 << apart) for i in range(lax.axis_size(axis))])


def in_blocks(array, dim, peers):
    dims = array.shape
    blocks = array.reshape(*dims[:dim], peers, dims[dim] // peers, *dims[dim + 1 :])
    return jnp.moveaxis(blocks, dim, 0)


def sent_and_summed(array, axis, dim):
    peers = lax.axis_size(axis)
    blocks = lax.all_to_all(in_blocks(array, dim, peers), axis, 0, 0, tiled=True)
    return jnp.sum(blocks.astype(jnp.float32), axis=0)


def unit_rows(matrix, head_count, head_size):
    shaped = matrix.astype(jnp.float32).reshape(matrix.shape[0], head_count, head_size)
    return (shaped / jnp.sqrt(jnp.sum(shaped * shaped, axis=-1, keepdims=True) + epsilon)).astype(
        jnp.bfloat16
    )


def local(queries, keys, values, level_weights, out_weight):
    tok_rows, width = queries.shape
    head_count = level_weights.shape[0]
    head_size = width // head_count
    block_count = tok_rows // BLOCK
    local_levels = block_count.bit_length() - 1
    seq_levels = lax.axis_size("seq").bit_length() - 1
    q_unit = unit_rows(queries, head_count, head_size)
    k_unit = unit_rows(keys, head_count, head_size)
    v_rows = values.reshape(tok_rows, head_count, head_size)
    q_blocks = q_unit.reshape(block_count, BLOCK, head_count, head_size)
    k_blocks = k_unit.reshape(block_count, BLOCK, head_count, head_size)
    v_blocks = v_rows.reshape(block_count, BLOCK, head_count, head_size)
    scores = jnp.einsum("bihd,bjhd->bhij", q_blocks, k_blocks, preferred_element_type=jnp.float32)
    row_pos = jnp.arange(BLOCK, dtype=jnp.int32)
    causal = row_pos[:, None] >= row_pos[None, :]
    level_zero = level_weights[:, 0, :].reshape(head_count, block_count, BLOCK).transpose(1, 0, 2)
    weights = jnp.where(causal[None, None], scores * level_zero[..., None], 0.0).astype(
        jnp.bfloat16
    )
    totals = jnp.einsum("bhij,bjhd->bihd", weights, v_blocks, preferred_element_type=jnp.float32)
    states = jnp.einsum("bjhd,bjhe->bhde", k_blocks, v_blocks, preferred_element_type=jnp.float32)
    for level_idx in range(1, local_levels + 1):
        span_size = 2 ** (level_idx - 1)
        group_count = block_count // (2 * span_size)
        left_sum = (
            states.reshape(group_count, 2, span_size, head_count, head_size, head_size)[:, 0]
            .sum(axis=1)
            .astype(jnp.bfloat16)
        )
        right_rows = q_blocks.reshape(group_count, 2, span_size * BLOCK, head_count, head_size)[
            :, 1
        ]
        read_out = jnp.einsum(
            "gihd,ghde->gihe", right_rows, left_sum, preferred_element_type=jnp.float32
        )
        factor = (
            level_weights[:, level_idx, :]
            .reshape(head_count, group_count, 2, span_size * BLOCK)[:, :, 1]
            .transpose(1, 2, 0)
        )
        read_out = read_out * factor[..., None]
        totals = totals + jnp.stack([jnp.zeros_like(read_out), read_out], axis=1).reshape(
            block_count, BLOCK, head_count, head_size
        )
    own_state = states.sum(axis=0)
    position = lax.axis_index("seq")
    group_sum = own_state
    collected = []
    for level_idx in range(1, seq_levels + 1):
        partner = partner_2(group_sum.astype(jnp.bfloat16), "seq", level_idx - 1).astype(
            group_sum.dtype
        )
        is_upper = jnp.right_shift(position, level_idx - 1) & 1 == 1
        collected.append(jnp.where(is_upper, partner, 0.0))
        group_sum = group_sum + partner
    siblings = jnp.stack(collected)
    sibling_bf = siblings.astype(jnp.bfloat16)
    far_reads = jnp.einsum("thd,lhde->lthe", q_unit, sibling_bf, preferred_element_type=jnp.float32)
    far_factor = level_weights[:, local_levels + 1 : local_levels + 1 + seq_levels, :].transpose(
        1, 2, 0
    )
    attended = totals.reshape(tok_rows, head_count, head_size) + jnp.sum(
        far_reads * far_factor[..., None], axis=0
    )
    normed = attended / jnp.sqrt(jnp.mean(attended * attended, axis=-1, keepdims=True) + epsilon)
    normed = normed.astype(jnp.bfloat16).reshape(tok_rows, head_count * head_size)
    product = jnp.dot(normed, out_weight, preferred_element_type=jnp.float32)
    summed = sent_and_summed(product.astype(jnp.bfloat16), "head", 1)
    return summed.astype(jnp.bfloat16)


def solution(mesh):
    in_specs = (
        P("seq", "head"),
        P("seq", "head"),
        P("seq", "head"),
        P("head", None, "seq"),
        P("head", None),
    )
    out_specs = P("seq", "head")
    return jax.shard_map(local, mesh=mesh, in_specs=in_specs, out_specs=out_specs, check_vma=False)
```

profile of v0, /device:TPU:1, one launch (start us, length us, event | category | flops | bytes accessed | tf_op | source)
XLA Modules:
  0.0 171.2 jit_solution(331549466066088421)
XLA Ops:
  3.9 1.9 %copy.76 = f32[4,128,8,128]{1,3,2,0:T(8,128)} copy(f32[4,128,8,128]{3,2,1,0:T(8,128)S(1)} %bitcast.160) | data formatting | bytes 4194304 | tf_op jit(solution)/shard_map/reshape | solution.py:29
  5.8 2.1 %copy.123 = f32[64,8,8,128]{3,2,1,0:T(8,128)S(1)} copy(f32[64,8,8,128]{3,1,2,0:T(8,128)} %fusion.1) | data formatting | bytes 4194304
  8.7 3.9 %fusion.50 = (f32[8,128,128]{2,1,0:T(8,128)S(1)}, bf16[4,8,128,128]{3,2,1,0:T(8,128)(2,1)}, f32[4,8,128,128]{3,2,1,0:T(8,128)}) fusion(bf16[4,128,8,128]{3,2,1,0:T(8,128)(2,1)S(1)} %bitcast.170, f32[4,128,8,128]{1,3,2,0:T(8,128)} %copy.76, f32[4,128,8]{1,2,0:T(8,128)S(1)} %copy.75), kind=kOutput, calls=%fused_computation.85 | convolution fusion | flops 136183808 | bytes 6832128 | tf_op jit(solution)/shard_map/bjhd,bjhe->bhde/dot_general | solution.py:56
  13.5 3.2 %collective-permute-start = (bf16[8,128,128]{1,2,0:T(8,128)(2,1)}, bf16[8,128,128]{1,2,0:T(8,128)(2,1)S(1)}, u32[]{:S(2)}, u32[]{:S(2)}) collective-permute-start(bf16[8,128,128]{1,2,0:T(8,128)(2,1)} %convert_element_type.96), channel_id=1, source_target_pairs={{0,4},{4,0},{8,12},{12,8},{16,20},{20,16},{24,28},{28,24},{32,36},... | collective-permute-start | bytes 786440 | tf_op jit(solution)/shard_map/ppermute | solution.py:13
  22.4 2.8 %fusion.8 = f32[1,1,256,8,128]{2,4,3,1,0:T(8,128)} fusion(f32[256,8]{0,1:T(8,128)} %slice_bitcast_fusion.4, f32[1,1,256,8,128]{4,3,2,1,0:T(8,128)} %slice.46, f32[1,256,8]{1,2,0:T(8,128)} %copy.157, bf16[8,128,128]{2,1,0:T(8,128)(2,1)S(1)} %slice_reduce_fusion), kind=kOutput, calls=%fused_computation.25 | convolution fusion | flops 67895296 | bytes 2375680 | tf_op jit(solution)/shard_map/gihd,ghde->gihe/dot_general | solution.py:68
  25.2 2.5 %copy.116 = f32[1,1,256,8,128]{4,3,2,1,0:T(8,128)} copy(f32[1,1,256,8,128]{2,4,3,1,0:T(8,128)} %fusion.8) | data formatting | bytes 2097152
  27.7 2.7 %stack.43.clone = f32[1,2,256,8,128]{4,3,2,1,0:T(8,128)} pad(f32[1,1,256,8,128]{4,3,2,1,0:T(8,128)} %copy.116, f32[]{:T(128)} %constant.12.clone.1), padding=0_0x1_0x0_0x0_0x0_0 | pad | bytes 3145732 | tf_op jit(solution)/shard_map/stack | solution.py:77
  30.4 2.9 %copy.90 = f32[4,128,8,128]{1,3,2,0:T(8,128)} copy(f32[4,128,8,128]{3,2,1,0:T(8,128)} %bitcast.161) | data formatting | bytes 4194304 | tf_op jit(solution)/shard_map/reshape | solution.py:77
  34.4 2.1 %fusion.6 = f32[2,1,128,8,128]{2,4,3,1,0:T(8,128)S(1)} fusion(bf16[2,2,1,8,128,128]{5,4,3,1,0,2:T(8,128)(2,1)} %bitcast.176, f32[2,128,8]{1,2,0:T(8,128)S(1)} %slice_bitcast_fusion.5, f32[2,1,128,8,128]{4,3,2,1,0:T(8,128)} %slice.42, f32[2,1,128,8]{2,3,0,1:T(8,128)S(1)} %copy.158), kind=kOutput, calls=%fused_computation.23 | convolution fusion | flops 67895296 | bytes 2637824 | tf_op jit(solution)/shard_map/gihd,ghde->gihe/dot_general | solution.py:68
  39.6 6.2 %fusion.3 = f32[4,128,8,128]{1,3,2,0:T(8,128)} fusion(f32[4,128,8,128]{1,3,2,0:T(8,128)} %copy.90, f32[2,2,128,8,128]{2,4,3,1,0:T(8,128)} %stack.41.clone, f32[4,8,128]{2,1,0:T(8,128)} %get-tuple-element.9, f32[4,128,8,128]{3,2,1,0:T(8,128)S(1)} %bitcast.156, f32[4,128,8]{1,2,0:T(8,128)} %copy.73, pred[128,128]{1,0:T(8,128)(4,1)} %iota_compare_fusion, ...), kind=kOutput, calls=%fused_computation.11 | convolution fusion | flops 273154048 | bytes 11599872 | tf_op jit(solution)/shard_map/bhij,bjhd->bihd/dot_general | solution.py:55
  51.4 5.8 %collective-permute-done.2 = bf16[8,128,128]{1,2,0:T(8,128)(2,1)S(1)} collective-permute-done((bf16[8,128,128]{1,2,0:T(8,128)(2,1)S(1)}, bf16[8,128,128]{1,2,0:T(8,128)(2,1)S(1)}, u32[]{:S(2)}, u32[]{:S(2)}) %collective-permute-start.2) | collective-permute-done | bytes 262176 | tf_op jit(solution)/shard_map/ppermute | solution.py:13
  57.7 3.0 %copy.91 = f32[4,128,8,128]{3,2,1,0:T(8,128)} copy(f32[4,128,8,128]{1,3,2,0:T(8,128)} %fusion.3) | data formatting | bytes 4194304 | tf_op jit(solution)/shard_map/add | solution.py:77
  60.7 3.0 %collective-permute-done.3 = bf16[8,128,128]{1,2,0:T(8,128)(2,1)S(1)} collective-permute-done((bf16[8,128,128]{1,2,0:T(8,128)(2,1)S(1)}, bf16[8,128,128]{1,2,0:T(8,128)(2,1)S(1)}, u32[]{:S(2)}, u32[]{:S(2)}) %collective-permute-start.3) | collective-permute-done | bytes 262176 | tf_op jit(solution)/shard_map/ppermute | solution.py:13
  66.7 11.7 %collective-permute-done.4 = bf16[8,128,128]{1,2,0:T(8,128)(2,1)S(1)} collective-permute-done((bf16[8,128,128]{1,2,0:T(8,128)(2,1)S(1)}, bf16[8,128,128]{1,2,0:T(8,128)(2,1)S(1)}, u32[]{:S(2)}, u32[]{:S(2)}) %collective-permute-start.4) | collective-permute-done | bytes 262176 | tf_op jit(solution)/shard_map/ppermute | solution.py:13
  78.5 5.1 %collective-permute-start.5 = (bf16[8,128,128]{1,2,0:T(8,128)(2,1)S(1)}, bf16[8,128,128]{1,2,0:T(8,128)(2,1)S(1)}, u32[]{:S(2)}, u32[]{:S(2)}) collective-permute-start(bf16[8,128,128]{1,2,0:T(8,128)(2,1)S(1)} %fusion.27), channel_id=1, source_target_pairs={{0,128},{4,132},{8,136},{12,140},{16,144},{20,148},{24,152},{28,15... | collective-permute-start | bytes 786440 | tf_op jit(solution)/shard_map/ppermute | solution.py:13
  83.8 11.4 %collective-permute-done.5 = bf16[8,128,128]{1,2,0:T(8,128)(2,1)S(1)} collective-permute-done((bf16[8,128,128]{1,2,0:T(8,128)(2,1)S(1)}, bf16[8,128,128]{1,2,0:T(8,128)(2,1)S(1)}, u32[]{:S(2)}, u32[]{:S(2)}) %collective-permute-start.5) | collective-permute-done | bytes 262176 | tf_op jit(solution)/shard_map/ppermute | solution.py:13
  95.3 1.8 %fusion = f32[512,8,128]{0,2,1:T(8,128)S(1)} fusion(f32[6,512,8]{1,0,2:T(8,128)S(1)} %copy.100, bf16[6,8,128,128]{2,3,0,1:T(8,128)(2,1)S(1)} %fusion.35, bf16[512,8,128,1]{2,1,0,3:T(8,128)(2,1)S(1)} %copy-done.8), kind=kOutput, calls=%fused_computation.1 | convolution fusion | flops 811073536 | bytes 4816896 | tf_op jit(solution)/shard_map/thd,lhde->lthe/dot_general | solution.py:93
  97.2 2.1 %copy.102 = f32[512,8,128]{2,1,0:T(8,128)} copy(f32[512,8,128]{0,2,1:T(8,128)S(1)} %fusion) | data formatting | bytes 4194304 | tf_op jit(solution)/shard_map/reduce_sum | solution.py:97
  99.3 3.0 %copy.103 = f32[4,128,8,128]{1,3,2,0:T(8,128)} copy(f32[4,128,8,128]{3,2,1,0:T(8,128)} %bitcast.162) | data formatting | bytes 4194304 | tf_op jit(solution)/shard_map/reduce_sum | solution.py:97
  102.3 2.0 %multiply_reduce_fusion = f32[4,128,8]{1,2,0:T(8,128)S(1)} fusion(f32[4,128,8,128]{1,3,2,0:T(8,128)S(1)} %copy-done, f32[4,128,8,128]{1,3,2,0:T(8,128)} %copy.103), kind=kLoop, calls=%fused_computation.14 | loop fusion | flops 1568768 | bytes 4210688 | tf_op jit(solution)/shard_map/reduce_sum | solution.py:100
  104.5 1.9 %copy.101 = f32[512,1024]{1,0:T(8,128)S(1)} copy(f32[512,1024]{0,1:T(8,128)} %bitcast.159) | data formatting | bytes 4194304 | tf_op jit(solution)/shard_map/reduce_sum | solution.py:97
  108.0 8.3 %convolution_convert_fusion = bf16[512,4096]{1,0:T(8,128)(2,1)S(1)} fusion(bf16[1024,4096]{1,0:T(8,128)(2,1)} %param.9, f32[64,8,8,128]{3,2,1,0:T(8,128)S(1)} %bitcast.167, f32[512,1024]{1,0:T(8,128)S(1)} %copy.101, f32[64,8,8,128]{3,2,1,0:T(8,128)S(1)} %bitcast.168), kind=kOutput, calls=%fused_computation.2 | convolution fusion | flops 4298637312 | bytes 18874368 | tf_op jit(solution)/shard_map/dot_general | solution.py:102
  116.8 49.9 %all_to_all.5 = bf16[4,512,1024]{2,1,0:T(8,128)(2,1)} all-to-all(bf16[4,512,1024]{2,1,0:T(8,128)(2,1)S(1)} %bitcast.157), channel_id=1, replica_groups=mesh['seq'=64,'head'=4] {'head'}, dimensions={0} | all-to-all | bytes 8388608 | tf_op jit(solution)/shard_map/all_to_all | solution.py:24
  166.8 4.4 %reduce_sum.82 = bf16[512,1024]{1,0:T(8,128)(2,1)} reduce(bf16[4,512,1024]{2,1,0:T(8,128)(2,1)} %all_to_all.5, bf16[]{:T(256)} %constant.28.clone.1), dimensions={0}, to_apply=%region_6.7 | reduce | flops 1572864 | bytes 5242882 | tf_op jit(solution)/shard_map/reduce_sum | solution.py:25
  (76 shorter events, 27.0 us)
Async XLA Ops:
  0.0 1.6 copy-start.2
  1.6 1.6 copy-start.7
  3.5 5.2 %copy-start.9 = (bf16[64,8,8,128]{3,2,1,0:T(8,128)(2,1)}, bf16[64,8,8,128]{3,2,1,0:T(8,128)(2,1)S(1)}, u32[]{:S(2)}) copy-start(bf16[64,8,8,128]{3,2,1,0:T(8,128)(2,1)S(1)} %copy.124) | copy-start | bytes 3145732
  8.7 3.9 %copy-start.12 = (f32[4,128,8]{1,2,0:T(8,128)}, f32[4,128,8]{1,2,0:T(8,128)S(1)}, u32[]{:S(2)}) copy-start(f32[4,128,8]{1,2,0:T(8,128)S(1)} %copy.75) | copy-start | bytes 49156
  8.7 8.0 %copy-start.10 = (f32[8,9,512]{2,0,1:T(8,128)S(1)}, f32[8,9,512]{2,0,1:T(8,128)}, u32[]{:S(2)}) copy-start(f32[8,9,512]{2,0,1:T(8,128)} %param.8) | copy-start | bytes 442372
  12.5 5.4 %copy-start.6 = (bf16[512,1024]{1,0:T(8,128)(2,1)S(1)}, bf16[512,1024]{1,0:T(8,128)(2,1)}, u32[]{:S(2)}) copy-start(bf16[512,1024]{1,0:T(8,128)(2,1)} %param.5) | copy-start | bytes 3145732
  13.5 25.9 %collective-permute-start = (bf16[8,128,128]{1,2,0:T(8,128)(2,1)}, bf16[8,128,128]{1,2,0:T(8,128)(2,1)S(1)}, u32[]{:S(2)}, u32[]{:S(2)}) collective-permute-start(bf16[8,128,128]{1,2,0:T(8,128)(2,1)} %convert_element_type.96), channel_id=1, source_target_pairs={{0,4},{4,0},{8,12},{12,8},{16,20},{20,16},{24,28},{28,24},{32,36},... | collective-permute-start | bytes 786440 | tf_op jit(solution)/shard_map/ppermute | solution.py:13
  30.4 2.9 %copy-start.11 = (f32[8,1,512]{2,0,1:T(8,128)S(1)}, f32[8,1,512]{2,0,1:T(8,128)}, u32[]{:S(2)}) copy-start(f32[8,1,512]{2,0,1:T(8,128)} %get-tuple-element.10) | copy-start | bytes 49156
  39.4 6.3 %copy-start.3 = (bf16[8,128,128]{1,2,0:T(8,128)(2,1)}, bf16[8,128,128]{1,2,0:T(8,128)(2,1)S(1)}, u32[]{:S(2)}) copy-start(bf16[8,128,128]{1,2,0:T(8,128)(2,1)S(1)} %collective-permute-done) | copy-start | bytes 786436
  39.5 8.1 %collective-permute-start.1 = (bf16[8,128,128]{1,2,0:T(8,128)(2,1)S(1)}, bf16[8,128,128]{1,2,0:T(8,128)(2,1)}, u32[]{:S(2)}, u32[]{:S(2)}) collective-permute-start(bf16[8,128,128]{1,2,0:T(8,128)(2,1)S(1)} %fusion.32), channel_id=1, source_target_pairs={{0,8},{4,12},{8,0},{12,4},{16,24},{20,28},{24,16},{28,20},{32,40},... | collective-permute-start | bytes 786440 | tf_op jit(solution)/shard_map/ppermute | solution.py:13
  48.7 8.6 %collective-permute-start.2 = (bf16[8,128,128]{1,2,0:T(8,128)(2,1)S(1)}, bf16[8,128,128]{1,2,0:T(8,128)(2,1)S(1)}, u32[]{:S(2)}, u32[]{:S(2)}) collective-permute-start(bf16[8,128,128]{1,2,0:T(8,128)(2,1)S(1)} %get-tuple-element.5), channel_id=1, source_target_pairs={{0,16},{4,20},{8,24},{12,28},{16,0},{20,4},{24,8},{28,12},{32,48},... | collective-permute-start | bytes 786440 | tf_op jit(solution)/shard_map/ppermute | solution.py:13
  57.3 6.4 %collective-permute-start.3 = (bf16[8,128,128]{1,2,0:T(8,128)(2,1)S(1)}, bf16[8,128,128]{1,2,0:T(8,128)(2,1)S(1)}, u32[]{:S(2)}, u32[]{:S(2)}) collective-permute-start(bf16[8,128,128]{1,2,0:T(8,128)(2,1)S(1)} %fusion.33), channel_id=1, source_target_pairs={{0,32},{4,36},{8,40},{12,44},{16,48},{20,52},{24,56},{28,60},{32,0... | collective-permute-start | bytes 786440 | tf_op jit(solution)/shard_map/ppermute | solution.py:13
  57.7 3.0 %copy-start.4 = (bf16[8,128,128]{1,2,0:T(8,128)(2,1)S(1)}, bf16[8,128,128]{1,2,0:T(8,128)(2,1)}, u32[]{:S(2)}) copy-start(bf16[8,128,128]{1,2,0:T(8,128)(2,1)} %copy-done.3) | copy-start | bytes 786436
  63.8 31.5 %copy-start.8 = (bf16[512,8,128,1]{2,1,0,3:T(8,128)(2,1)S(1)}, bf16[512,8,128,1]{2,1,0,3:T(8,128)(2,1)}, u32[]{:S(2)}) copy-start(bf16[512,8,128,1]{2,1,0,3:T(8,128)(2,1)} %fusion.17) | copy-start | bytes 3145732
  63.8 14.6 %collective-permute-start.4 = (bf16[8,128,128]{1,2,0:T(8,128)(2,1)S(1)}, bf16[8,128,128]{1,2,0:T(8,128)(2,1)S(1)}, u32[]{:S(2)}, u32[]{:S(2)}) collective-permute-start(bf16[8,128,128]{1,2,0:T(8,128)(2,1)S(1)} %fusion.47), channel_id=1, source_target_pairs={{0,64},{4,68},{8,72},{12,76},{16,80},{20,84},{24,88},{28,92},{32,9... | collective-permute-start | bytes 786440 | tf_op jit(solution)/shard_map/ppermute | solution.py:13
  78.5 16.7 %collective-permute-start.5 = (bf16[8,128,128]{1,2,0:T(8,128)(2,1)S(1)}, bf16[8,128,128]{1,2,0:T(8,128)(2,1)S(1)}, u32[]{:S(2)}, u32[]{:S(2)}) collective-permute-start(bf16[8,128,128]{1,2,0:T(8,128)(2,1)S(1)} %fusion.27), channel_id=1, source_target_pairs={{0,128},{4,132},{8,136},{12,140},{16,144},{20,148},{24,152},{28,15... | collective-permute-start | bytes 786440 | tf_op jit(solution)/shard_map/ppermute | solution.py:13
  97.2 2.1 %copy-start.1 = (f32[512,8,128]{0,2,1:T(8,128)}, f32[512,8,128]{0,2,1:T(8,128)S(1)}, u32[]{:S(2)}) copy-start(f32[512,8,128]{0,2,1:T(8,128)S(1)} %fusion) | copy-start | bytes 6291460
  99.3 3.1 %copy-start = (f32[4,128,8,128]{1,3,2,0:T(8,128)S(1)}, f32[4,128,8,128]{1,3,2,0:T(8,128)}, u32[]{:S(2)}) copy-start(f32[4,128,8,128]{1,3,2,0:T(8,128)} %fusion.3) | copy-start | bytes 6291460
  106.4 1.6 copy-start.5
where the time goes:
time: 173 us; the launch traced here: 171 us
  blocking collectives  49.9 us (29%)
  waiting for transfers between devices  33.7 us (19%)
  local copies, waits for them, and re-layouts  32.1 us (19%)
  matrix products  25.1 us (15%)
  other arithmetic  18.4 us (11%)
  starting transfers between devices  11.5 us (7%)
    all_to_all x1, blocking collectives, sent_and_summed(): lax.all_to_all(in_blocks(array, dim, peers), axis, 0, 0, tiled=True)  49.9 us
    ppermute x6, waiting for transfers between devices, partner_2(): lax.ppermute(array, axis, [(i, i ^ 1 << apart) for i in range(lax.axis_si...  33.7 us
    ppermute x6, starting transfers between devices, partner_2(): lax.ppermute(array, axis, [(i, i ^ 1 << apart) for i in range(lax.axis_si...  11.5 us
    dot_general x1, matrix products, local(): product = jnp.dot(normed, out_weight, preferred_element_type=jnp.float32)  8.34 us
    unnamed x33, local copies, waits for them, and re-layouts  7.55 us
    reduce_sum x3, local copies, waits for them, and re-layouts, local(): jnp.sum(far_reads * far_factor[..., None], axis=0)  7.06 us
    dot_general x1, matrix products, local(): jnp.einsum('bhij,bjhd->bihd', weights, v_blocks, preferred_element_type=j...  6.18 us
    dot_general x2, matrix products, local(): jnp.einsum('gihd,ghde->gihe', right_rows, left_sum, preferred_element_typ...  4.92 us
  transfers between devices with their start and end apart: 6, of which 5 were waited for; matrix products, arithmetic and copies ran while one was open for 20% of the time, Pallas kernels for 0%

commit v1 on v0

v1 whole, which is shorter than its diff:
```python
import jax
import jax.numpy as jnp
from jax import lax
from jax.experimental import pallas as pl
from jax.experimental.pallas import tpu as pltpu
from jax.sharding import PartitionSpec as P

BLOCK = 128
EPS = 1e-06
LINE = 8
CHIPS = 4
PLANES = 8
FAR = 6
BF = jnp.bfloat16
F32 = jnp.float32
MESH = pl.DeviceIdType.MESH


def dot(a, b):
    return jnp.dot(a, b, preferred_element_type=F32)


def kernel(
    q_hbm,
    k_hbm,
    v_hbm,
    lw_hbm,
    w_hbm,
    out_ref,
    q_v,
    k_v,
    v_v,
    lw_v,
    w_v,
    bst,
    stbuf,
    recv1,
    lowbuf,
    zrecv,
    states,
    qs,
    tot,
    nrm,
    p1s,
    p1r,
    p2s,
    p2r,
    mine,
    own,
    in_sem,
    p1_s,
    p1_r,
    core_s,
    core_r,
    z_s,
    z_r,
    low_s,
    low_r,
    hi_s,
    hi_r,
    y1_s,
    y1_r,
    y2_s,
    y2_r,
):
    heads = stbuf.shape[0]
    tok = q_v.shape[0]
    nblk = tok // BLOCK
    p = lax.axis_index("seq")
    y = lax.axis_index("head")
    z = p // LINE
    d = p % LINE
    core = d % 2
    x = d // 2
    pa = y + 1 - 2 * (y % 2)
    pb = 3 - y
    opp = (y + 2) % 4

    def line(e):
        return (z * LINE + e, y)

    def local_in(i, src, dst):
        return pltpu.make_async_copy(src, dst, in_sem.at[i])

    cps = [
        local_in(0, k_hbm, k_v),
        local_in(1, v_hbm, v_v),
        local_in(2, q_hbm, q_v),
        local_in(3, lw_hbm, lw_v),
        local_in(4, w_hbm, w_v),
    ]
    for c in cps:
        c.start()

    barrier = pltpu.get_barrier_semaphore()
    for i in range(1, LINE):
        pl.semaphore_signal(barrier, inc=1, device_id=line((d + i) % LINE), device_id_type=MESH)
    for i in range(1, PLANES):
        pl.semaphore_signal(
            barrier, inc=1, device_id=(((z + i) % PLANES) * LINE + d, y), device_id_type=MESH
        )
    for t in (pa, pb):
        pl.semaphore_signal(barrier, inc=1, device_id=(p, t), device_id_type=MESH)

    def cols(h):
        return pl.ds(pl.multiple_of(h * 128, 128), 128)

    @pl.when(core == 0)
    def _():
        states[:, pl.ds(0, 128), :] = jnp.zeros((heads, 128, 128), BF)

    cps[0].wait()
    cps[1].wait()

    def key_head(h, _):
        kf = k_v[:, cols(h)].astype(F32)
        ku = (kf * lax.rsqrt(jnp.sum(kf * kf, axis=-1, keepdims=True) + EPS)).astype(BF)
        k_v[:, cols(h)] = ku
        vv = v_v[:, cols(h)]
        s = [
            lax.dot_general(
                ku[b * BLOCK : (b + 1) * BLOCK],
                vv[b * BLOCK : (b + 1) * BLOCK],
                (((0,), (0,)), ((), ())),
                preferred_element_type=F32,
            )
            for b in range(nblk)
        ]
        s01 = s[0] + s[1]
        bst[h, 0] = s[0].astype(BF)
        bst[h, 1] = s[2].astype(BF)
        bst[h, 2] = s01.astype(BF)
        stbuf[h] = (s01 + s[2] + s[3]).astype(BF)
        return 0

    lax.fori_loop(0, heads, key_head, 0)
    pl.semaphore_wait(barrier, LINE - 1 + PLANES - 1 + 2)

    def send1(e):
        return pltpu.make_async_remote_copy(
            src_ref=stbuf.at[e],
            dst_ref=recv1.at[d],
            send_sem=p1_s.at[e],
            recv_sem=p1_r.at[d],
            device_id=line(e),
            device_id_type=MESH,
        )

    for i in range(1, LINE):
        send1((d + i) % LINE).start()
    core_copy = pltpu.make_async_remote_copy(
        src_ref=stbuf,
        dst_ref=states.at[:, pl.ds(0, 128), :],
        send_sem=core_s,
        recv_sem=core_r,
        device_id=line(d + 1 - 2 * core),
        device_id_type=MESH,
    )

    @pl.when(core == 0)
    def _():
        core_copy.start()

    recv1[d] = stbuf[d]

    cps[2].wait()
    cps[3].wait()
    causal = lax.broadcasted_iota(jnp.int32, (BLOCK, BLOCK), 0) >= lax.broadcasted_iota(
        jnp.int32, (BLOCK, BLOCK), 1
    )

    def query_head(h, _):
        qf = q_v[:, cols(h)].astype(F32)
        qu = (qf * lax.rsqrt(jnp.sum(qf * qf, axis=-1, keepdims=True) + EPS)).astype(BF)
        q_v[:, cols(h)] = qu
        lwt = lw_v[h].T
        for b in range(nblk):
            rows = pl.ds(b * BLOCK, BLOCK)
            part = slice(b * BLOCK, (b + 1) * BLOCK)
            qb = qu[part]
            s = lax.dot_general(
                qb, k_v[rows, cols(h)], (((1,), (1,)), ((), ())), preferred_element_type=F32
            )
            wgt = jnp.where(causal, s * lwt[part, 0:1], 0.0).astype(BF)
            acc = dot(wgt, v_v[rows, cols(h)])
            if b % 2 == 1:
                acc = acc + dot(qb, bst[h, b // 2]) * lwt[part, 1:2]
            if b >= 2:
                acc = acc + dot(qb, bst[h, 2]) * lwt[part, 2:3]
            tot[rows, cols(h)] = acc
        return 0

    lax.fori_loop(0, heads, query_head, 0)

    for i in range(1, LINE):
        e = (d + i) % LINE
        pltpu.make_async_remote_copy(
            src_ref=stbuf.at[e],
            dst_ref=recv1.at[e],
            send_sem=p1_s.at[e],
            recv_sem=p1_r.at[e],
            device_id=line(e),
            device_id_type=MESH,
        ).wait_recv()
    pair = [recv1[2 * c].astype(F32) + recv1[2 * c + 1].astype(F32) for c in range(CHIPS)]
    half = pair[0] + pair[1]
    zrecv[z] = (half + pair[2] + pair[3]).astype(BF)

    def zsend(t):
        return pltpu.make_async_remote_copy(
            src_ref=zrecv.at[z],
            dst_ref=zrecv.at[z],
            send_sem=z_s.at[t],
            recv_sem=z_r.at[z],
            device_id=(t * LINE + d, y),
            device_id_type=MESH,
        )

    for t in range(1, PLANES):

        @pl.when(z < t)
        def _():
            zsend(t).start()

    none = jnp.zeros((128, 128), BF)
    for c in range(CHIPS):
        lowbuf[c, 0] = pair[c - 1].astype(BF) if c % 2 else none
        lowbuf[c, 1] = half.astype(BF) if c >= 2 else none

    low_rows = pl.ds(128, 256)
    hi_rows = pl.ds(384, 384)

    def spread(src, rows, peer, s_sem, i, r_sem, h):
        return pltpu.make_async_remote_copy(
            src_ref=src,
            dst_ref=states.at[h, rows, :],
            send_sem=s_sem.at[i],
            recv_sem=r_sem.at[h],
            device_id=line(peer),
            device_id_type=MESH,
        )

    mate = d + 1 - 2 * core
    sends = []
    states[d, pl.ds(128, 128), :] = lowbuf[x, 0]
    states[d, pl.ds(256, 128), :] = lowbuf[x, 1]
    lowsrc = lowbuf.reshape(CHIPS, 256, 128)
    for i in range(1, CHIPS):
        c = (x + i) % CHIPS
        cp = spread(lowsrc.at[c], low_rows, c * 2 + core, low_s, i, low_r, d)
        cp.start()
        sends.append(cp)
    cp = spread(lowsrc.at[x], low_rows, mate, low_s, 0, low_r, d)
    cp.start()
    sends.append(cp)

    def scale_head(h, _):
        quf = q_v[:, cols(h)].astype(F32)
        lwt = lw_v[h].T
        for lv in range(FAR):
            qs[h, :, lv * 128 : (lv + 1) * 128] = (quf * lwt[:, 3 + lv : 4 + lv]).astype(BF)
        return 0

    lax.fori_loop(0, heads, scale_head, 0)

    def forward(rows, s_sem, r_sem):
        for i in range(1, CHIPS):
            c = (x + CHIPS - i) % CHIPS
            h = c * 2 + core
            spread(states.at[h, rows, :], rows, mate, s_sem, 0, r_sem, h).wait_recv()
            cp = spread(states.at[h, rows, :], rows, mate, s_sem, CHIPS + i - 1, r_sem, h)
            cp.start()
            sends.append(cp)

    def landed(rows, s_sem, r_sem):
        for i in range(CHIPS):
            h = i * 2 + 1 - core
            spread(states.at[h, rows, :], rows, mate, s_sem, 0, r_sem, h).wait_recv()

    forward(low_rows, low_s, low_r)

    for s in range(PLANES - 1):

        @pl.when(s < z)
        def _():
            pltpu.make_async_remote_copy(
                src_ref=zrecv.at[s],
                dst_ref=zrecv.at[s],
                send_sem=z_s.at[0],
                recv_sem=z_r.at[s],
                device_id=(s * LINE + d, y),
                device_id_type=MESH,
            ).wait_recv()

    def put(row, val):
        states[d, pl.ds(row, 128), :] = val

    base = (z // 4) * 4

    @pl.when(z % 2 == 1)
    def _():
        put(384, zrecv[z - 1])

    @pl.when(z % 2 == 0)
    def _():
        put(384, none)

    @pl.when((z // 2) % 2 == 1)
    def _():
        put(512, (zrecv[base].astype(F32) + zrecv[base + 1].astype(F32)).astype(BF))

    @pl.when((z // 2) % 2 == 0)
    def _():
        put(512, none)

    @pl.when(z >= 4)
    def _():
        q4 = [zrecv[i].astype(F32) for i in range(4)]
        put(640, (q4[0] + q4[1] + q4[2] + q4[3]).astype(BF))

    @pl.when(z < 4)
    def _():
        put(640, none)

    mysrc = states.at[d, hi_rows, :]
    for i in range(1, CHIPS):
        c = (x + i) % CHIPS
        cp = spread(mysrc, hi_rows, c * 2 + core, hi_s, i, hi_r, d)
        cp.start()
        sends.append(cp)
    cp = spread(mysrc, hi_rows, mate, hi_s, 0, hi_r, d)
    cp.start()
    sends.append(cp)

    landed(low_rows, low_s, low_r)

    @pl.when(core == 1)
    def _():
        core_copy.wait_recv()

    def low_head(h, _):
        tot[:, cols(h)] += dot(qs[h, :, 0:384], states[h, 0:384, :])
        return 0

    lax.fori_loop(0, heads, low_head, 0)

    forward(hi_rows, hi_s, hi_r)
    landed(hi_rows, hi_s, hi_r)

    def norm_head(h, _):
        a = tot[:, cols(h)] + dot(qs[h, :, 384:768], states[h, 384:768, :])
        m = jnp.mean(a * a, axis=-1, keepdims=True)
        nrm[:, cols(h)] = (a * lax.rsqrt(m + EPS)).astype(BF)
        return 0

    lax.fori_loop(0, heads, norm_head, 0)
    cps[4].wait()

    top = tok // 2
    wide = out_ref.shape[1]
    tiles = mine.shape[1]
    tw = wide // tiles

    def tile_product(block, t):
        lo = pl.multiple_of(block * wide + t * tw, tw)
        return dot(nrm[...], w_v[:, pl.ds(lo, tw)])

    def y1(side, i):
        return pltpu.make_async_remote_copy(
            src_ref=p1s.at[side, i],
            dst_ref=p1r.at[side, i],
            send_sem=y1_s.at[side, i],
            recv_sem=y1_r.at[side, i],
            device_id=(p, (pa, pb)[side]),
            device_id_type=MESH,
        )

    def y2(side, i):
        return pltpu.make_async_remote_copy(
            src_ref=p2s.at[side, i],
            dst_ref=p2r.at[side, i],
            send_sem=y2_s.at[side, i],
            recv_sem=y2_r.at[side, i],
            device_id=(p, (pa, pb)[side]),
            device_id_type=MESH,
        )

    def far_tile(t, _):
        prod = tile_product(opp, t)
        p1s[0, t] = prod[:top].astype(BF)
        y1(0, t).start()
        p1s[1, t] = prod[top:].astype(BF)
        y1(1, t).start()
        return 0

    lax.fori_loop(0, tiles, far_tile, 0)

    def side_tile(t, _):
        prod = tile_product(pa, t)
        p1s[0, tiles + t] = prod[:top].astype(BF)
        y1(0, tiles + t).start()
        mine[0, t] = prod[top:]
        prod = tile_product(pb, t)
        p1s[1, tiles + t] = prod[top:].astype(BF)
        y1(1, tiles + t).start()
        mine[1, t] = prod[:top]
        return 0

    lax.fori_loop(0, tiles, side_tile, 0)

    def second(t, _):
        y1(1, t).wait_recv()
        p2s[0, t] = (mine[0, t] + p1r[1, t].astype(F32)).astype(BF)
        y2(0, t).start()
        y1(0, t).wait_recv()
        p2s[1, t] = (mine[1, t] + p1r[0, t].astype(F32)).astype(BF)
        y2(1, t).start()
        return 0

    def own_tile(t, _):
        own[t] = tile_product(y, t)
        return 0

    lax.fori_loop(0, tiles, own_tile, 0)
    lax.fori_loop(0, tiles, second, 0)

    def last(t, _):
        lanes = pl.ds(pl.multiple_of(t * tw, tw), tw)
        y1(0, tiles + t).wait_recv()
        y2(1, t).wait_recv()
        out_ref[pl.ds(0, top), lanes] = (
            own[t, pl.ds(0, top), :] + p1r[0, tiles + t].astype(F32) + p2r[1, t].astype(F32)
        ).astype(BF)
        y1(1, tiles + t).wait_recv()
        y2(0, t).wait_recv()
        out_ref[pl.ds(top, top), lanes] = (
            own[t, pl.ds(top, top), :] + p1r[1, tiles + t].astype(F32) + p2r[0, t].astype(F32)
        ).astype(BF)
        return 0

    lax.fori_loop(0, tiles, last, 0)

    for i in range(1, LINE):
        send1((d + i) % LINE).wait_send()

    @pl.when(core == 0)
    def _():
        core_copy.wait_send()

    for t in range(1, PLANES):

        @pl.when(z < t)
        def _():
            zsend(t).wait_send()

    for cp in sends:
        cp.wait_send()
    for side in range(2):

        def drain(i, _):
            y1(side, i).wait_send()
            return 0

        lax.fori_loop(0, 2 * tiles, drain, 0)

        def drain2(i, _):
            y2(side, i).wait_send()
            return 0

        lax.fori_loop(0, tiles, drain2, 0)


def local(queries, keys, values, level_weights, out_weight):
    tok, width = queries.shape
    heads, levels, _ = level_weights.shape
    tiles = 4
    top = tok // 2
    tw = width // tiles
    dma = pltpu.SemaphoreType.DMA
    scratch = [
        pltpu.VMEM((tok, width), BF),
        pltpu.VMEM((tok, width), BF),
        pltpu.VMEM((tok, width), BF),
        pltpu.VMEM((heads, levels, tok), F32),
        pltpu.VMEM(out_weight.shape, BF),
        pltpu.VMEM((heads, 3, 128, 128), BF),
        pltpu.VMEM((heads, 128, 128), BF),
        pltpu.VMEM((LINE, 128, 128), BF),
        pltpu.VMEM((CHIPS, 2, 128, 128), BF),
        pltpu.VMEM((PLANES, 128, 128), BF),
        pltpu.VMEM((heads, FAR * 128, 128), BF),
        pltpu.VMEM((heads, tok, FAR * 128), BF),
        pltpu.VMEM((tok, width), F32),
        pltpu.VMEM((tok, width), BF),
        pltpu.VMEM((2, 2 * tiles, top, tw), BF),
        pltpu.VMEM((2, 2 * tiles, top, tw), BF),
        pltpu.VMEM((2, tiles, top, tw), BF),
        pltpu.VMEM((2, tiles, top, tw), BF),
        pltpu.VMEM((2, tiles, top, tw), F32),
        pltpu.VMEM((tiles, tok, tw), F32),
        dma((5,)),
        dma((LINE,)),
        dma((LINE,)),
        dma,
        dma,
        dma((PLANES,)),
        dma((PLANES,)),
        dma((2 * CHIPS,)),
        dma((LINE,)),
        dma((2 * CHIPS,)),
        dma((LINE,)),
        dma((2, 2 * tiles)),
        dma((2, 2 * tiles)),
        dma((2, tiles)),
        dma((2, tiles)),
    ]
    return pl.pallas_call(
        kernel,
        out_shape=jax.ShapeDtypeStruct((tok, width), BF),
        in_specs=[pl.BlockSpec(memory_space=pl.ANY)] * 5,
        out_specs=pl.BlockSpec(memory_space=pltpu.VMEM),
        scratch_shapes=scratch,
        compiler_params=pltpu.CompilerParams(
            collective_id=0, has_side_effects=True, vmem_limit_bytes=60 * 1024 * 1024
        ),
    )(queries, keys, values, level_weights, out_weight)


def solution(mesh):
    in_specs = (
        P("seq", "head"),
        P("seq", "head"),
        P("seq", "head"),
        P("head", None, "seq"),
        P("head", None),
    )
    out_specs = P("seq", "head")
    return jax.shard_map(local, mesh=mesh, in_specs=in_specs, out_specs=out_specs, check_vma=False)
```

time: 173 us -> 74.3 us (0.43)
  Pallas kernels: 0 us -> 70.2 us
  blocking collectives: 49.9 us -> 0 us
  waiting for transfers between devices: 33.7 us -> 0 us
  local copies, waits for them, and re-layouts: 32.1 us -> 3.97 us
  matrix products: 25.1 us -> 0 us
  other arithmetic: 18.4 us -> 0 us
  starting transfers between devices: 11.5 us -> 0 us
    pallas_call x0 -> x1, Pallas kernels: none -> 70.2 us  [local(): pl.pallas_call(kernel, out_shape=jax.ShapeDtypeStruct((tok, width), BF),...]
    all_to_all x1 -> x0, blocking collectives: 49.9 us -> none  [sent_and_summed(): lax.all_to_all(in_blocks(array, dim, peers), axis, 0, 0, tiled=True)]
    ppermute x6 -> x0, waiting for transfers between devices: 33.7 us -> none  [partner_2(): lax.ppermute(array, axis, [(i, i ^ 1 << apart) for i in range(lax.axis_si...]
    dot_general x6 -> x0, matrix products: 25.1 us -> none  [the longest x1 8.34 us: local(): product = jnp.dot(normed, out_weight, preferred_element_type=jnp.float32)]
    ppermute x6 -> x0, starting transfers between devices: 11.5 us -> none  [partner_2(): lax.ppermute(array, axis, [(i, i ^ 1 << apart) for i in range(lax.axis_si...]
    reduce_sum x5 -> x0, other arithmetic: 8.96 us -> none  [the longest x1 4.39 us: sent_and_summed(): return jnp.sum(blocks.astype(jnp.float32), axis=0)]
    reduce_sum x4 -> x0, local copies, waits for them, and re-layouts: 7.26 us -> none  [the longest x3 7.06 us: local(): jnp.sum(far_reads * far_factor[..., None], axis=0)]
    reshape x3 -> x0, local copies, waits for them, and re-layouts: 5.24 us -> none  [the longest x1 2.93 us: local(): jnp.stack([jnp.zeros_like(read_out), read_out], axis=1)]
  transfers between devices with their start and end apart: 6 -> 0, of which waited for: 5 -> 0; matrix products, arithmetic and copies ran while one was open for 20% -> 0% of each run, Pallas kernels for 0% -> 0%
where the time goes in v1:
time: 74.3 us; the launch traced here: 74.1 us
  Pallas kernels  70.2 us (94%)
  local copies, waits for them, and re-layouts  3.97 us (5%)
    pallas_call x1, Pallas kernels, local(): pl.pallas_call(kernel, out_shape=jax.ShapeDtypeStruct((tok, width), BF),...  70.2 us
    unnamed x2, local copies, waits for them, and re-layouts  3.97 us

profile of v1, /device:TPU:1, one launch (start us, length us, event | category | flops | bytes accessed | tf_op | source)
XLA Modules:
  0.0 74.1 jit_solution(11161501208027204905)
XLA Ops:
  0.0 1.7 %copy.6.lw_hbm = f32[8,9,512]{2,1,0:T(8,128)} copy(f32[8,9,512]{2,0,1:T(8,128)} %param.8) | data formatting | bytes 294912 | tf_op args[3]
  1.7 70.2 %shard_map.55 = bf16[512,1024]{1,0:T(8,128)(2,1)} custom-call(bf16[512,1024]{1,0:T(8,128)(2,1)} %q_hbm.1, bf16[512,1024]{1,0:T(8,128)(2,1)} %k_hbm.1, bf16[512,1024]{1,0:T(8,128)(2,1)} %v_hbm.1, f32[8,9,512]{2,1,0:T(8,128)} %copy.6.lw_hbm, bf16[1024,4096]{1,0:T(8,128)(2,1)} %w_hbm.1), custom_call_target="tpu_custom_call" | custom-call | tf_op jit(solution)/shard_map/pallas_call | solution.py:517
  71.9 2.3 %copy.8 = bf16[512,1024]{1,0:T(8,128)(2,1)} copy(bf16[512,1024]{1,0:T(8,128)(2,1)} %shard_map.55) | data formatting | bytes 2097152

commit v2 on v1

--- a/solution.py
+++ b/solution.py
@@ -11,6 +11,9 @@
 CHIPS = 4
 PLANES = 8
 FAR = 6
+NEAR = (1, 2, 3, PLANES - 3, PLANES - 2, PLANES - 1)
+TAKERS = {0: (3, 2, 1), 1: (3, 2, 0), 2: (3, 0), 3: (0,), 4: (7, 6, 5), 5: (7, 6), 6: (7,)}
+ROOTS = {3: (5, 4), 0: (6, 7)}
 BF = jnp.bfloat16
 F32 = jnp.float32
 MESH = pl.DeviceIdType.MESH
@@ -31,6 +34,7 @@
     k_v,
     v_v,
     lw_v,
+    lw_t,
     w_v,
     bst,
     stbuf,
@@ -56,6 +60,8 @@
     z_r,
     low_s,
     low_r,
+    mid_s,
+    mid_r,
     hi_s,
     hi_r,
     y1_s,
@@ -95,7 +101,7 @@
     barrier = pltpu.get_barrier_semaphore()
     for i in range(1, LINE):
         pl.semaphore_signal(barrier, inc=1, device_id=line((d + i) % LINE), device_id_type=MESH)
-    for i in range(1, PLANES):
+    for i in NEAR:
         pl.semaphore_signal(
             barrier, inc=1, device_id=(((z + i) % PLANES) * LINE + d, y), device_id_type=MESH
         )
@@ -108,6 +114,14 @@
     @pl.when(core == 0)
     def _():
         states[:, pl.ds(0, 128), :] = jnp.zeros((heads, 128, 128), BF)
+
+    @pl.when(x % 2 == 0)
+    def _():
+        states[:, pl.ds(128, 128), :] = jnp.zeros((heads, 128, 128), BF)
+
+    @pl.when(x < 2)
+    def _():
+        states[:, pl.ds(256, 128), :] = jnp.zeros((heads, 128, 128), BF)
 
     cps[0].wait()
     cps[1].wait()
@@ -133,8 +147,8 @@
         stbuf[h] = (s01 + s[2] + s[3]).astype(BF)
         return 0
 
-    lax.fori_loop(0, heads, key_head, 0)
-    pl.semaphore_wait(barrier, LINE - 1 + PLANES - 1 + 2)
+    lax.fori_loop(0, heads, key_head, 0, unroll=True)
+    pl.semaphore_wait(barrier, LINE - 1 + len(NEAR) + 2)
 
     def send1(e):
         return pltpu.make_async_remote_copy(
@@ -165,6 +179,12 @@
 
     cps[2].wait()
     cps[3].wait()
+    lw_all = lw_v[...].reshape(lw_v.shape[0] * heads, tok)
+    lw_t[...] = jnp.concatenate([lw_all, jnp.zeros((128 - lw_all.shape[0], tok), F32)], axis=0).T
+
+    def level_columns(h):
+        return pltpu.roll(lw_t[...], lax.rem(128 - h, 128), 1)
+
     causal = lax.broadcasted_iota(jnp.int32, (BLOCK, BLOCK), 0) >= lax.broadcasted_iota(
         jnp.int32, (BLOCK, BLOCK), 1
     )
@@ -173,7 +193,7 @@
         qf = q_v[:, cols(h)].astype(F32)
         qu = (qf * lax.rsqrt(jnp.sum(qf * qf, axis=-1, keepdims=True) + EPS)).astype(BF)
         q_v[:, cols(h)] = qu
-        lwt = lw_v[h].T
+        lwt = level_columns(h)
         for b in range(nblk):
             rows = pl.ds(b * BLOCK, BLOCK)
             part = slice(b * BLOCK, (b + 1) * BLOCK)
@@ -184,13 +204,13 @@
             wgt = jnp.where(causal, s * lwt[part, 0:1], 0.0).astype(BF)
             acc = dot(wgt, v_v[rows, cols(h)])
             if b % 2 == 1:
-                acc = acc + dot(qb, bst[h, b // 2]) * lwt[part, 1:2]
+                acc = acc + dot(qb, bst[h, b // 2]) * lwt[part, 8:9]
             if b >= 2:
-                acc = acc + dot(qb, bst[h, 2]) * lwt[part, 2:3]
+                acc = acc + dot(qb, bst[h, 2]) * lwt[part, 16:17]
             tot[rows, cols(h)] = acc
         return 0
 
-    lax.fori_loop(0, heads, query_head, 0)
+    lax.fori_loop(0, heads, query_head, 0, unroll=True)
 
     for i in range(1, LINE):
         e = (d + i) % LINE
@@ -206,29 +226,30 @@
     half = pair[0] + pair[1]
     zrecv[z] = (half + pair[2] + pair[3]).astype(BF)
 
-    def zsend(t):
+    def zcopy(slot, src, t):
         return pltpu.make_async_remote_copy(
-            src_ref=zrecv.at[z],
-            dst_ref=zrecv.at[z],
-            send_sem=z_s.at[t],
-            recv_sem=z_r.at[z],
+            src_ref=zrecv.at[src],
+            dst_ref=zrecv.at[src],
+            send_sem=z_s.at[slot],
+            recv_sem=z_r.at[src],
             device_id=(t * LINE + d, y),
             device_id_type=MESH,
         )
 
-    for t in range(1, PLANES):
-
-        @pl.when(z < t)
-        def _():
-            zsend(t).start()
+    for src, takers in TAKERS.items():
+
+        @pl.when(z == src)
+        def _():
+            for slot, t in enumerate(takers):
+                zcopy(slot, src, t).start()
 
     none = jnp.zeros((128, 128), BF)
     for c in range(CHIPS):
-        lowbuf[c, 0] = pair[c - 1].astype(BF) if c % 2 else none
-        lowbuf[c, 1] = half.astype(BF) if c >= 2 else none
-
-    low_rows = pl.ds(128, 256)
-    hi_rows = pl.ds(384, 384)
+        lowbuf[c, pl.ds(0, 128), :] = pair[c - 1].astype(BF) if c % 2 else none
+        lowbuf[c, pl.ds(128, 128), :] = half.astype(BF) if c >= 2 else none
+
+    mid_rows = pl.ds(384, 256)
+    hi_rows = pl.ds(640, 128)
 
     def spread(src, rows, peer, s_sem, i, r_sem, h):
         return pltpu.make_async_remote_copy(
@@ -242,33 +263,76 @@
 
     mate = d + 1 - 2 * core
     sends = []
-    states[d, pl.ds(128, 128), :] = lowbuf[x, 0]
-    states[d, pl.ds(256, 128), :] = lowbuf[x, 1]
-    lowsrc = lowbuf.reshape(CHIPS, 256, 128)
-    for i in range(1, CHIPS):
-        c = (x + i) % CHIPS
-        cp = spread(lowsrc.at[c], low_rows, c * 2 + core, low_s, i, low_r, d)
-        cp.start()
-        sends.append(cp)
-    cp = spread(lowsrc.at[x], low_rows, mate, low_s, 0, low_r, d)
-    cp.start()
-    sends.append(cp)
-
-    def scale_head(h, _):
+    states[d, pl.ds(128, 256), :] = lowbuf[x]
+    def low_copy(c, slot):
+        first = 0 if c % 2 else 1
+        count = 2 if c == 3 else 1
+        return pltpu.make_async_remote_copy(
+            src_ref=lowbuf.at[c, pl.ds(first * 128, count * 128), :],
+            dst_ref=states.at[d, pl.ds(128 + first * 128, count * 128), :],
+            send_sem=low_s.at[slot],
+            recv_sem=low_r.at[d],
+            device_id=line(mate if slot == 0 else c * 2 + core),
+            device_id_type=MESH,
+        )
+
+    for c in range(1, CHIPS):
+
+        @pl.when(x != c)
+        def _():
+            low_copy(c, c).start()
+
+        @pl.when(x == c)
+        def _():
+            low_copy(c, 0).start()
+
+    def scaled(h, levels):
         quf = q_v[:, cols(h)].astype(F32)
-        lwt = lw_v[h].T
-        for lv in range(FAR):
-            qs[h, :, lv * 128 : (lv + 1) * 128] = (quf * lwt[:, 3 + lv : 4 + lv]).astype(BF)
-        return 0
-
-    lax.fori_loop(0, heads, scale_head, 0)
+        lwt = level_columns(h)
+        for lv in levels:
+            col = 8 * (3 + lv)
+            qs[h, :, lv * 128 : (lv + 1) * 128] = (quf * lwt[:, col : col + 1]).astype(BF)
+        return 0
+
+    def scale_low(h, _):
+        return scaled(h, range(0, 3))
+
+    def scale_high(h, _):
+        return scaled(h, range(3, FAR))
+
+    lax.fori_loop(0, heads, scale_low, 0, unroll=True)
+
+    def low_forward(c):
+        first = 0 if c % 2 else 1
+        count = 2 if c == 3 else 1
+        rows = pl.ds(128 + first * 128, count * 128)
+        for i in range(1, CHIPS):
+            h = ((c + i) % CHIPS) * 2 + core
+            spread(states.at[h, rows, :], rows, mate, low_s, 0, low_r, h).wait_recv()
+            spread(states.at[h, rows, :], rows, mate, low_s, CHIPS + i - 1, low_r, h).start()
+
+    def low_landed(c):
+        first = 0 if c % 2 else 1
+        count = 2 if c == 3 else 1
+        rows = pl.ds(128 + first * 128, count * 128)
+        for i in range(CHIPS):
+            h = i * 2 + 1 - core
+            spread(states.at[h, rows, :], rows, mate, low_s, 0, low_r, h).wait_recv()
+
+    def along_line(rows, s_sem, r_sem):
+        src = states.at[d, rows, :]
+        for i in (2, 1, 3, 0):
+            e = ((x + i) % CHIPS) * 2 + core if i else mate
+            cp = spread(src, rows, e, s_sem, i, r_sem, d)
+            cp.start()
+            sends.append(cp)
 
     def forward(rows, s_sem, r_sem):
-        for i in range(1, CHIPS):
-            c = (x + CHIPS - i) % CHIPS
-            h = c * 2 + core
-            spread(states.at[h, rows, :], rows, mate, s_sem, 0, r_sem, h).wait_recv()
-            cp = spread(states.at[h, rows, :], rows, mate, s_sem, CHIPS + i - 1, r_sem, h)
+        for i in (1, 3, 2):
+            h = ((x + i) % CHIPS) * 2 + core
+            src = states.at[h, rows, :]
+            spread(src, rows, mate, s_sem, 0, r_sem, h).wait_recv()
+            cp = spread(src, rows, mate, s_sem, 3 + i, r_sem, h)
             cp.start()
             sends.append(cp)
 
@@ -277,24 +341,26 @@
             h = i * 2 + 1 - core
             spread(states.at[h, rows, :], rows, mate, s_sem, 0, r_sem, h).wait_recv()
 
-    forward(low_rows, low_s, low_r)
-
-    for s in range(PLANES - 1):
-
-        @pl.when(s < z)
-        def _():
-            pltpu.make_async_remote_copy(
-                src_ref=zrecv.at[s],
-                dst_ref=zrecv.at[s],
-                send_sem=z_s.at[0],
-                recv_sem=z_r.at[s],
-                device_id=(s * LINE + d, y),
-                device_id_type=MESH,
-            ).wait_recv()
+    for t in range(PLANES):
+
+        @pl.when(z == t)
+        def _():
+            for src, takers in TAKERS.items():
+                if t in takers:
+                    zcopy(0, src, t).wait_recv()
 
     def put(row, val):
         states[d, pl.ds(row, 128), :] = val
 
+    for root, takers in ROOTS.items():
+
+        @pl.when(z == root)
+        def _():
+            q4 = [zrecv[i].astype(F32) for i in range(4)]
+            zrecv[PLANES] = (q4[0] + q4[1] + q4[2] + q4[3]).astype(BF)
+            for slot, t in enumerate(takers):
+                zcopy(3 + slot, PLANES, t).start()
+
     base = (z // 4) * 4
 
     @pl.when(z % 2 == 1)
@@ -313,26 +379,29 @@
     def _():
         put(512, none)
 
+    along_line(mid_rows, mid_s, mid_r)
+    lax.fori_loop(0, heads, scale_high, 0, unroll=True)
+    for c in range(1, CHIPS):
+
+        @pl.when(x == c)
+        def _():
+            low_forward(c)
+
     @pl.when(z >= 4)
     def _():
-        q4 = [zrecv[i].astype(F32) for i in range(4)]
-        put(640, (q4[0] + q4[1] + q4[2] + q4[3]).astype(BF))
+        zcopy(0, PLANES, 0).wait_recv()
+        put(640, zrecv[PLANES])
 
     @pl.when(z < 4)
     def _():
         put(640, none)
 
-    mysrc = states.at[d, hi_rows, :]
-    for i in range(1, CHIPS):
-        c = (x + i) % CHIPS
-        cp = spread(mysrc, hi_rows, c * 2 + core, hi_s, i, hi_r, d)
-        cp.start()
-        sends.append(cp)
-    cp = spread(mysrc, hi_rows, mate, hi_s, 0, hi_r, d)
-    cp.start()
-    sends.append(cp)
-
-    landed(low_rows, low_s, low_r)
+    along_line(hi_rows, hi_s, hi_r)
+    for c in range(1, CHIPS):
+
+        @pl.when(x == c)
+        def _():
+            low_landed(c)
 
     @pl.when(core == 1)
     def _():
@@ -342,18 +411,27 @@
         tot[:, cols(h)] += dot(qs[h, :, 0:384], states[h, 0:384, :])
         return 0
 
-    lax.fori_loop(0, heads, low_head, 0)
+    lax.fori_loop(0, heads, low_head, 0, unroll=True)
+
+    forward(mid_rows, mid_s, mid_r)
+    landed(mid_rows, mid_s, mid_r)
+
+    def mid_head(h, _):
+        tot[:, cols(h)] += dot(qs[h, :, 384:640], states[h, 384:640, :])
+        return 0
+
+    lax.fori_loop(0, heads, mid_head, 0, unroll=True)
 
     forward(hi_rows, hi_s, hi_r)
     landed(hi_rows, hi_s, hi_r)
 
     def norm_head(h, _):
-        a = tot[:, cols(h)] + dot(qs[h, :, 384:768], states[h, 384:768, :])
+        a = tot[:, cols(h)] + dot(qs[h, :, 640:768], states[h, 640:768, :])
         m = jnp.mean(a * a, axis=-1, keepdims=True)
         nrm[:, cols(h)] = (a * lax.rsqrt(m + EPS)).astype(BF)
         return 0
 
-    lax.fori_loop(0, heads, norm_head, 0)
+    lax.fori_loop(0, heads, norm_head, 0, unroll=True)
     cps[4].wait()
 
     top = tok // 2
@@ -447,11 +525,31 @@
     def _():
         core_copy.wait_send()
 
-    for t in range(1, PLANES):
-
-        @pl.when(z < t)
-        def _():
-            zsend(t).wait_send()
+    for src in range(PLANES):
+
+        @pl.when(z == src)
+        def _():
+            for slot, t in enumerate(TAKERS.get(src, ())):
+                zcopy(slot, src, t).wait_send()
+            for slot, t in enumerate(ROOTS.get(src, ())):
+                zcopy(3 + slot, PLANES, t).wait_send()
+
+    for c in range(1, CHIPS):
+
+        @pl.when(x != c)
+        def _():
+            low_copy(c, c).wait_send()
+
+        @pl.when(x == c)
+        def _():
+            low_copy(c, 0).wait_send()
+            first = 0 if c % 2 else 1
+            count = 2 if c == 3 else 1
+            rows = pl.ds(128 + first * 128, count * 128)
+            for i in range(1, CHIPS):
+                spread(
+                    states.at[0, rows, :], rows, mate, low_s, CHIPS + i - 1, low_r, 0
+                ).wait_send()
 
     for cp in sends:
         cp.wait_send()
@@ -481,13 +579,14 @@
         pltpu.VMEM((tok, width), BF),
         pltpu.VMEM((tok, width), BF),
         pltpu.VMEM((tok, width), BF),
-        pltpu.VMEM((heads, levels, tok), F32),
+        pltpu.VMEM((levels, heads, tok), F32),
+        pltpu.VMEM((tok, 128), F32),
         pltpu.VMEM(out_weight.shape, BF),
         pltpu.VMEM((heads, 3, 128, 128), BF),
         pltpu.VMEM((heads, 128, 128), BF),
         pltpu.VMEM((LINE, 128, 128), BF),
-        pltpu.VMEM((CHIPS, 2, 128, 128), BF),
-        pltpu.VMEM((PLANES, 128, 128), BF),
+        pltpu.VMEM((CHIPS, 256, 128), BF),
+        pltpu.VMEM((PLANES + 1, 128, 128), BF),
         pltpu.VMEM((heads, FAR * 128, 128), BF),
         pltpu.VMEM((heads, tok, FAR * 128), BF),
         pltpu.VMEM((tok, width), F32),
@@ -503,8 +602,10 @@
         dma((LINE,)),
         dma,
         dma,
-        dma((PLANES,)),
-        dma((PLANES,)),
+        dma((5,)),
+        dma((PLANES + 1,)),
+        dma((2 * CHIPS,)),
+        dma((LINE,)),
         dma((2 * CHIPS,)),
         dma((LINE,)),
         dma((2 * CHIPS,)),
@@ -516,14 +617,14 @@
     ]
     return pl.pallas_call(
         kernel,
-        out_shape=jax.ShapeDtypeStruct((tok, width), BF),
+        out_shape=pltpu.VMEM((tok, width), BF),
         in_specs=[pl.BlockSpec(memory_space=pl.ANY)] * 5,
         out_specs=pl.BlockSpec(memory_space=pltpu.VMEM),
         scratch_shapes=scratch,
         compiler_params=pltpu.CompilerParams(
             collective_id=0, has_side_effects=True, vmem_limit_bytes=60 * 1024 * 1024
         ),
-    )(queries, keys, values, level_weights, out_weight)
+    )(queries, keys, values, level_weights.transpose(1, 0, 2), out_weight)
 
 
 def solution(mesh):

time: 74.3 us -> 66.9 us (0.900)
  Pallas kernels: 70.2 us -> 65.9 us
  local copies, waits for them, and re-layouts: 3.97 us -> 0.97 us
    pallas_call x1, Pallas kernels: 70.2 us -> 65.9 us  [local(): pl.pallas_call(kernel, out_shape=pltpu.VMEM((tok, width), BF), in_specs=[...]
    unnamed x2 -> x1, local copies, waits for them, and re-layouts: 3.97 us -> 0.97 us
where the time goes in v2:
time: 66.9 us; the launch traced here: 66.8 us
  Pallas kernels  65.9 us (99%)
  local copies, waits for them, and re-layouts  0.97 us (1%)
    pallas_call x1, Pallas kernels, local(): pl.pallas_call(kernel, out_shape=pltpu.VMEM((tok, width), BF), in_specs=[...  65.9 us

profile of v2, /device:TPU:1, one launch (start us, length us, event | category | flops | bytes accessed | tf_op | source)
XLA Modules:
  0.0 66.8 jit_solution(16346572455192319527)
XLA Ops:
  0.0 65.9 %shard_map.55 = bf16[512,1024]{1,0:T(8,128)(2,1)S(1)} custom-call(bf16[512,1024]{1,0:T(8,128)(2,1)} %q_hbm.1, bf16[512,1024]{1,0:T(8,128)(2,1)} %k_hbm.1, bf16[512,1024]{1,0:T(8,128)(2,1)} %v_hbm.1, f32[9,8,512]{2,1,0:T(8,128)} %bitcast.1, bf16[1024,4096]{1,0:T(8,128)(2,1)} %w_hbm.1), custom_call_target="tpu_custom_call" | custom-call | tf_op jit(solution)/shard_map/pallas_call | solution.py:618
  65.9 1.0 %copy.7 = bf16[512,1024]{1,0:T(8,128)(2,1)} copy(bf16[512,1024]{1,0:T(8,128)(2,1)S(1)} %shard_map.55) | data formatting | bytes 2097152

commit v3 on v2

--- a/solution.py
+++ b/solution.py
@@ -51,6 +51,11 @@
     p2r,
     mine,
     own,
+    wp,
+    pn,
+    h2s,
+    h2r,
+    ownh,
     in_sem,
     p1_s,
     p1_r,
@@ -68,6 +73,13 @@
     y1_r,
     y2_s,
     y2_r,
+    wf_s,
+    w_s,
+    w_r,
+    hy_s,
+    hy_r,
+    h2_s,
+    h2_r,
 ):
     heads = stbuf.shape[0]
     tok = q_v.shape[0]
@@ -162,6 +174,24 @@
 
     for i in range(1, LINE):
         send1((d + i) % LINE).start()
+
+    share = w_hbm.shape[0] // LINE
+    width = out_ref.shape[1]
+    my_rows = pl.ds(pl.multiple_of(d * share, share), share)
+
+    def w_fetch(j):
+        block = (pa, opp)[j]
+        return pltpu.make_async_remote_copy(
+            src_ref=w_hbm.at[my_rows, pl.ds(pl.multiple_of(block * width, width), width)],
+            dst_ref=wp.at[j, my_rows, :],
+            send_sem=wf_s.at[j],
+            recv_sem=w_r.at[d, j],
+            device_id=(p, pa),
+            device_id_type=MESH,
+        )
+
+    for j in range(2):
+        w_fetch(j).start()
     core_copy = pltpu.make_async_remote_copy(
         src_ref=stbuf,
         dst_ref=states.at[:, pl.ds(0, 128), :],
@@ -420,6 +450,31 @@
         tot[:, cols(h)] += dot(qs[h, :, 384:640], states[h, 384:640, :])
         return 0
 
+    ahead = (x + 1 + 2 * core) % CHIPS
+    behind = (x + 3 - 2 * core) % CHIPS
+
+    def w_move(h, j, peer, slot):
+        rows = pl.ds(pl.multiple_of(h * share, share), share)
+        return pltpu.make_async_remote_copy(
+            src_ref=wp.at[j, rows, :],
+            dst_ref=wp.at[j, rows, :],
+            send_sem=w_s.at[slot, j],
+            recv_sem=w_r.at[h, j],
+            device_id=line(peer),
+            device_id_type=MESH,
+        )
+
+    def w_send(h, j, peer, slot):
+        cp = w_move(h, j, peer, slot)
+        cp.start()
+        sends.append(cp)
+
+    for j in range(2):
+        w_move(d, j, mate, 0).wait_recv()
+        w_send(d, j, ahead * 2 + core, 0)
+        w_send(d, j, behind * 2 + core, 1)
+        w_send(d, j, mate, 2)
+
     lax.fori_loop(0, heads, mid_head, 0, unroll=True)
 
     forward(hi_rows, hi_s, hi_r)
@@ -434,14 +489,16 @@
     lax.fori_loop(0, heads, norm_head, 0, unroll=True)
     cps[4].wait()
 
-    top = tok // 2
-    wide = out_ref.shape[1]
+    top = p1s.shape[2]
+    lead = 2 * top
     tiles = mine.shape[1]
-    tw = wide // tiles
+    tw = width // tiles
+
+    def w_tile(block, t):
+        return w_v[:, pl.ds(pl.multiple_of(block * width + t * tw, tw), tw)]
 
     def tile_product(block, t):
-        lo = pl.multiple_of(block * wide + t * tw, tw)
-        return dot(nrm[...], w_v[:, pl.ds(lo, tw)])
+        return dot(nrm[pl.ds(0, lead), :], w_tile(block, t))
 
     def y1(side, i):
         return pltpu.make_async_remote_copy(
@@ -472,6 +529,21 @@
         return 0
 
     lax.fori_loop(0, tiles, far_tile, 0)
+    part = pn.shape[1]
+    parts = pn.shape[0]
+
+    def normed_copy(c):
+        return pltpu.make_async_remote_copy(
+            src_ref=nrm.at[pl.ds(lead + c * part, part), :],
+            dst_ref=pn.at[c],
+            send_sem=hy_s.at[c],
+            recv_sem=hy_r.at[c],
+            device_id=(p, pa),
+            device_id_type=MESH,
+        )
+
+    for c in range(parts):
+        normed_copy(c).start()
 
     def side_tile(t, _):
         prod = tile_product(pa, t)
@@ -499,8 +571,57 @@
         own[t] = tile_product(y, t)
         return 0
 
+    for j in range(2):
+        h = behind * 2 + core
+        w_move(h, j, mate, 0).wait_recv()
+        w_send(h, j, ahead * 2 + core, 3)
+        w_send(h, j, mate, 4)
+    for j in range(2):
+        h = ahead * 2 + core
+        w_move(h, j, mate, 0).wait_recv()
+        w_send(h, j, mate, 5)
     lax.fori_loop(0, tiles, own_tile, 0)
     lax.fori_loop(0, tiles, second, 0)
+    for j in range(2):
+        h = ((x + 2) % CHIPS) * 2 + core
+        w_move(h, j, mate, 0).wait_recv()
+        w_send(h, j, mate, 6)
+    for j in range(2):
+        for i in range(CHIPS):
+            w_move(i * 2 + 1 - core, j, mate, 0).wait_recv()
+
+    def h2(c, t):
+        return pltpu.make_async_remote_copy(
+            src_ref=h2s.at[c, t],
+            dst_ref=h2r.at[c, t],
+            send_sem=h2_s.at[c, t],
+            recv_sem=h2_r.at[c, t],
+            device_id=(p, pb),
+            device_id_type=MESH,
+        )
+
+    def both(c, block, j, t):
+        lanes = pl.ds(pl.multiple_of(t * tw, tw), tw)
+        own_rows = nrm[pl.ds(lead + c * part, part), :]
+        return dot(own_rows, w_tile(block, t)) + dot(pn[c], wp[j, :, lanes])
+
+    for c in range(parts):
+        normed_copy(c).wait_recv()
+
+        def give_tile(t, _):
+            h2s[c, t] = both(c, pb, 1, t).astype(BF)
+            h2(c, t).start()
+            return 0
+
+        lax.fori_loop(0, tiles, give_tile, 0)
+
+    for c in range(parts):
+
+        def keep_tile(t, _):
+            ownh[c, t] = both(c, y, 0, t)
+            return 0
+
+        lax.fori_loop(0, tiles, keep_tile, 0)
 
     def last(t, _):
         lanes = pl.ds(pl.multiple_of(t * tw, tw), tw)
@@ -517,6 +638,28 @@
         return 0
 
     lax.fori_loop(0, tiles, last, 0)
+    for c in range(parts):
+
+        def last_given(t, _):
+            lanes = pl.ds(pl.multiple_of(t * tw, tw), tw)
+            h2(c, t).wait_recv()
+            out_ref[pl.ds(lead + c * part, part), lanes] = (
+                ownh[c, t] + h2r[c, t].astype(F32)
+            ).astype(BF)
+            return 0
+
+        lax.fori_loop(0, tiles, last_given, 0)
+
+    for j in range(2):
+        w_fetch(j).wait_send()
+    for c in range(parts):
+        normed_copy(c).wait_send()
+
+        def drain3(t, _):
+            h2(c, t).wait_send()
+            return 0
+
+        lax.fori_loop(0, tiles, drain3, 0)
 
     for i in range(1, LINE):
         send1((d + i) % LINE).wait_send()
@@ -572,7 +715,9 @@
     tok, width = queries.shape
     heads, levels, _ = level_weights.shape
     tiles = 4
-    top = tok // 2
+    top = tok // 4
+    parts = 2
+    part = (tok - 2 * top) // parts
     tw = width // tiles
     dma = pltpu.SemaphoreType.DMA
     scratch = [
@@ -596,7 +741,12 @@
         pltpu.VMEM((2, tiles, top, tw), BF),
         pltpu.VMEM((2, tiles, top, tw), BF),
         pltpu.VMEM((2, tiles, top, tw), F32),
-        pltpu.VMEM((tiles, tok, tw), F32),
+        pltpu.VMEM((tiles, 2 * top, tw), F32),
+        pltpu.VMEM((2, width, width), BF),
+        pltpu.VMEM((parts, part, width), BF),
+        pltpu.VMEM((parts, tiles, part, tw), BF),
+        pltpu.VMEM((parts, tiles, part, tw), BF),
+        pltpu.VMEM((parts, tiles, part, tw), F32),
         dma((5,)),
         dma((LINE,)),
         dma((LINE,)),
@@ -614,6 +764,13 @@
         dma((2, 2 * tiles)),
         dma((2, tiles)),
         dma((2, tiles)),
+        dma((2,)),
+        dma((7, 2)),
+        dma((LINE, 2)),
+        dma((parts,)),
+        dma((parts,)),
+        dma((parts, tiles)),
+        dma((parts, tiles)),
     ]
     return pl.pallas_call(
         kernel,

time: 66.9 us -> 62.2 us (0.930)
  Pallas kernels: 65.9 us -> 61.2 us
    pallas_call x1, Pallas kernels: 65.9 us -> 61.2 us  [local(): pl.pallas_call(kernel, out_shape=pltpu.VMEM((tok, width), BF), in_specs=[...]
where the time goes in v3:
time: 62.2 us
  Pallas kernels  61.2 us (98%)
  local copies, waits for them, and re-layouts  0.97 us (2%)
    pallas_call x1, Pallas kernels, local(): pl.pallas_call(kernel, out_shape=pltpu.VMEM((tok, width), BF), in_specs=[...  61.2 us

profile of v3, /device:TPU:1, one launch (start us, length us, event | category | flops | bytes accessed | tf_op | source)
XLA Modules:
  0.0 62.2 jit_solution(13002784709261309600)
XLA Ops:
  0.0 61.2 %shard_map.55 = bf16[512,1024]{1,0:T(8,128)(2,1)S(1)} custom-call(bf16[512,1024]{1,0:T(8,128)(2,1)} %q_hbm.1, bf16[512,1024]{1,0:T(8,128)(2,1)} %k_hbm.1, bf16[512,1024]{1,0:T(8,128)(2,1)} %v_hbm.1, f32[9,8,512]{2,1,0:T(8,128)} %bitcast.1, bf16[1024,4096]{1,0:T(8,128)(2,1)} %w_hbm.1), custom_call_target="tpu_custom_call" | custom-call | tf_op jit(solution)/shard_map/pallas_call | solution.py:775
  61.2 1.0 %copy.7 = bf16[512,1024]{1,0:T(8,128)(2,1)} copy(bf16[512,1024]{1,0:T(8,128)(2,1)S(1)} %shard_map.55) | data formatting | bytes 2097152

commit v4 on v3

--- a/solution.py
+++ b/solution.py
@@ -11,6 +11,7 @@
 CHIPS = 4
 PLANES = 8
 FAR = 6
+DIRECT = 256
 NEAR = (1, 2, 3, PLANES - 3, PLANES - 2, PLANES - 1)
 TAKERS = {0: (3, 2, 1), 1: (3, 2, 0), 2: (3, 0), 3: (0,), 4: (7, 6, 5), 5: (7, 6), 6: (7,)}
 ROOTS = {3: (5, 4), 0: (6, 7)}
@@ -172,26 +173,36 @@
             device_id_type=MESH,
         )
 
-    for i in range(1, LINE):
-        send1((d + i) % LINE).start()
-
-    share = w_hbm.shape[0] // LINE
+    for i in (2, 1, 3):
+        for c in range(2):
+            send1(((x + i) % CHIPS) * 2 + c).start()
+    send1(d + 1 - 2 * core).start()
+
+    share = (w_hbm.shape[0] - DIRECT) // LINE
     width = out_ref.shape[1]
-    my_rows = pl.ds(pl.multiple_of(d * share, share), share)
-
-    def w_fetch(j):
+
+    def w_rows(h):
+        return pl.ds(pl.multiple_of(DIRECT + h * share, 16), share)
+
+    def chip_rows(c):
+        return pl.ds(pl.multiple_of(c * (DIRECT // 2), 16), DIRECT // 2)
+
+    def w_fetch(i):
+        j = i % 2
         block = (pa, opp)[j]
-        return pltpu.make_async_remote_copy(
-            src_ref=w_hbm.at[my_rows, pl.ds(pl.multiple_of(block * width, width), width)],
-            dst_ref=wp.at[j, my_rows, :],
-            send_sem=wf_s.at[j],
-            recv_sem=w_r.at[d, j],
+        rows, piece = (w_rows(d), d) if i < 2 else (chip_rows(core), LINE + core)
+        return pltpu.make_async_remote_copy(
+            src_ref=w_hbm.at[rows, pl.ds(pl.multiple_of(block * width, width), width)],
+            dst_ref=wp.at[j, rows, :],
+            send_sem=wf_s.at[i],
+            recv_sem=w_r.at[piece, j],
             device_id=(p, pa),
             device_id_type=MESH,
         )
 
-    for j in range(2):
-        w_fetch(j).start()
+    fetches = 4 if DIRECT else 2
+    for i in range(fetches):
+        w_fetch(i).start()
     core_copy = pltpu.make_async_remote_copy(
         src_ref=stbuf,
         dst_ref=states.at[:, pl.ds(0, 128), :],
@@ -453,8 +464,8 @@
     ahead = (x + 1 + 2 * core) % CHIPS
     behind = (x + 3 - 2 * core) % CHIPS
 
-    def w_move(h, j, peer, slot):
-        rows = pl.ds(pl.multiple_of(h * share, share), share)
+    def w_move(h, j, peer, slot, rows=None):
+        rows = w_rows(h) if rows is None else rows
         return pltpu.make_async_remote_copy(
             src_ref=wp.at[j, rows, :],
             dst_ref=wp.at[j, rows, :],
@@ -475,22 +486,28 @@
         w_send(d, j, behind * 2 + core, 1)
         w_send(d, j, mate, 2)
 
+    forward(hi_rows, hi_s, hi_r)
     lax.fori_loop(0, heads, mid_head, 0, unroll=True)
 
-    forward(hi_rows, hi_s, hi_r)
     landed(hi_rows, hi_s, hi_r)
-
-    def norm_head(h, _):
-        a = tot[:, cols(h)] + dot(qs[h, :, 640:768], states[h, 640:768, :])
-        m = jnp.mean(a * a, axis=-1, keepdims=True)
-        nrm[:, cols(h)] = (a * lax.rsqrt(m + EPS)).astype(BF)
-        return 0
-
-    lax.fori_loop(0, heads, norm_head, 0, unroll=True)
-    cps[4].wait()
 
     top = p1s.shape[2]
     lead = 2 * top
+
+    def normalize(lo, n):
+        rows = pl.ds(lo, n)
+
+        def norm_head(h, _):
+            a = tot[rows, cols(h)] + dot(qs[h, rows, 640:768], states[h, 640:768, :])
+            m = jnp.mean(a * a, axis=-1, keepdims=True)
+            nrm[rows, cols(h)] = (a * lax.rsqrt(m + EPS)).astype(BF)
+            return 0
+
+        lax.fori_loop(0, heads, norm_head, 0, unroll=True)
+
+    normalize(0, lead)
+    cps[4].wait()
+
     tiles = mine.shape[1]
     tw = width // tiles
 
@@ -543,6 +560,7 @@
         )
 
     for c in range(parts):
+        normalize(lead + c * part, part)
         normed_copy(c).start()
 
     def side_tile(t, _):
@@ -571,6 +589,12 @@
         own[t] = tile_product(y, t)
         return 0
 
+    if DIRECT:
+        for j in range(2):
+            w_move(LINE + core, j, mate, 7, chip_rows(core)).wait_recv()
+            cp = w_move(LINE + core, j, mate, 7, chip_rows(core))
+            cp.start()
+            sends.append(cp)
     for j in range(2):
         h = behind * 2 + core
         w_move(h, j, mate, 0).wait_recv()
@@ -589,6 +613,8 @@
     for j in range(2):
         for i in range(CHIPS):
             w_move(i * 2 + 1 - core, j, mate, 0).wait_recv()
+        if DIRECT:
+            w_move(LINE + 1 - core, j, mate, 0, chip_rows(1 - core)).wait_recv()
 
     def h2(c, t):
         return pltpu.make_async_remote_copy(
@@ -650,8 +676,8 @@
 
         lax.fori_loop(0, tiles, last_given, 0)
 
-    for j in range(2):
-        w_fetch(j).wait_send()
+    for i in range(fetches):
+        w_fetch(i).wait_send()
     for c in range(parts):
         normed_copy(c).wait_send()
 
@@ -715,7 +741,7 @@
     tok, width = queries.shape
     heads, levels, _ = level_weights.shape
     tiles = 4
-    top = tok // 4
+    top = 96
     parts = 2
     part = (tok - 2 * top) // parts
     tw = width // tiles
@@ -764,9 +790,9 @@
         dma((2, 2 * tiles)),
         dma((2, tiles)),
         dma((2, tiles)),
-        dma((2,)),
-        dma((7, 2)),
-        dma((LINE, 2)),
+        dma((4,)),
+        dma((8, 2)),
+        dma((LINE + 2, 2)),
         dma((parts,)),
         dma((parts,)),
         dma((parts, tiles)),

time: 62.2 us -> 60.8 us (0.977)
  Pallas kernels: 61.2 us -> 59.8 us
    pallas_call x1, Pallas kernels: 61.2 us -> 59.8 us  [local(): pl.pallas_call(kernel, out_shape=pltpu.VMEM((tok, width), BF), in_specs=[...]
where the time goes in v4:
time: 60.8 us; the launch traced here: 60.7 us
  Pallas kernels  59.8 us (98%)
  local copies, waits for them, and re-layouts  0.97 us (2%)
    pallas_call x1, Pallas kernels, local(): pl.pallas_call(kernel, out_shape=pltpu.VMEM((tok, width), BF), in_specs=[...  59.8 us

profile of v4, /device:TPU:1, one launch (start us, length us, event | category | flops | bytes accessed | tf_op | source)
XLA Modules:
  0.0 60.7 jit_solution(8030642154674703094)
XLA Ops:
  0.0 59.8 %shard_map.55 = bf16[512,1024]{1,0:T(8,128)(2,1)S(1)} custom-call(bf16[512,1024]{1,0:T(8,128)(2,1)} %q_hbm.1, bf16[512,1024]{1,0:T(8,128)(2,1)} %k_hbm.1, bf16[512,1024]{1,0:T(8,128)(2,1)} %v_hbm.1, f32[9,8,512]{2,1,0:T(8,128)} %bitcast.1, bf16[1024,4096]{1,0:T(8,128)(2,1)} %w_hbm.1), custom_call_target="tpu_custom_call" | custom-call | tf_op jit(solution)/shard_map/pallas_call | solution.py:801
  59.8 1.0 %copy.7 = bf16[512,1024]{1,0:T(8,128)(2,1)} copy(bf16[512,1024]{1,0:T(8,128)(2,1)S(1)} %shard_map.55) | data formatting | bytes 2097152

commit v5 on v4

--- a/solution.py
+++ b/solution.py
@@ -108,8 +108,8 @@
         local_in(3, lw_hbm, lw_v),
         local_in(4, w_hbm, w_v),
     ]
-    for c in cps:
-        c.start()
+    cps[0].start()
+    cps[1].start()
 
     barrier = pltpu.get_barrier_semaphore()
     for i in range(1, LINE):
@@ -138,6 +138,8 @@
 
     cps[0].wait()
     cps[1].wait()
+    cps[2].start()
+    cps[3].start()
 
     def key_head(h, _):
         kf = k_v[:, cols(h)].astype(F32)
@@ -200,6 +202,7 @@
             device_id_type=MESH,
         )
 
+    cps[4].start()
     fetches = 4 if DIRECT else 2
     for i in range(fetches):
         w_fetch(i).start()
@@ -455,12 +458,6 @@
     lax.fori_loop(0, heads, low_head, 0, unroll=True)
 
     forward(mid_rows, mid_s, mid_r)
-    landed(mid_rows, mid_s, mid_r)
-
-    def mid_head(h, _):
-        tot[:, cols(h)] += dot(qs[h, :, 384:640], states[h, 384:640, :])
-        return 0
-
     ahead = (x + 1 + 2 * core) % CHIPS
     behind = (x + 3 - 2 * core) % CHIPS
 
@@ -485,6 +482,12 @@
         w_send(d, j, ahead * 2 + core, 0)
         w_send(d, j, behind * 2 + core, 1)
         w_send(d, j, mate, 2)
+
+    landed(mid_rows, mid_s, mid_r)
+
+    def mid_head(h, _):
+        tot[:, cols(h)] += dot(qs[h, :, 384:640], states[h, 384:640, :])
+        return 0
 
     forward(hi_rows, hi_s, hi_r)
     lax.fori_loop(0, heads, mid_head, 0, unroll=True)

time: 60.8 us -> 60.2 us (level)
  Pallas kernels: 59.8 us -> 59.1 us
    pallas_call x1, Pallas kernels: 59.8 us -> 59.1 us  [local(): pl.pallas_call(kernel, out_shape=pltpu.VMEM((tok, width), BF), in_specs=[...]
where the time goes in v5:
time: 60.2 us; the launch traced here: 60.1 us
  Pallas kernels  59.1 us (98%)
  local copies, waits for them, and re-layouts  0.97 us (2%)
    pallas_call x1, Pallas kernels, local(): pl.pallas_call(kernel, out_shape=pltpu.VMEM((tok, width), BF), in_specs=[...  59.1 us

profile of v5, /device:TPU:1, one launch (start us, length us, event | category | flops | bytes accessed | tf_op | source)
XLA Modules:
  0.0 60.1 jit_solution(12579211561628132329)
XLA Ops:
  0.0 59.1 %shard_map.55 = bf16[512,1024]{1,0:T(8,128)(2,1)S(1)} custom-call(bf16[512,1024]{1,0:T(8,128)(2,1)} %q_hbm.1, bf16[512,1024]{1,0:T(8,128)(2,1)} %k_hbm.1, bf16[512,1024]{1,0:T(8,128)(2,1)} %v_hbm.1, f32[9,8,512]{2,1,0:T(8,128)} %bitcast.1, bf16[1024,4096]{1,0:T(8,128)(2,1)} %w_hbm.1), custom_call_target="tpu_custom_call" | custom-call | tf_op jit(solution)/shard_map/pallas_call | solution.py:804
  59.1 1.0 %copy.7 = bf16[512,1024]{1,0:T(8,128)(2,1)} copy(bf16[512,1024]{1,0:T(8,128)(2,1)S(1)} %shard_map.55) | data formatting | bytes 2097152

commit v6 on v5

--- a/solution.py
+++ b/solution.py
@@ -592,12 +592,6 @@
         own[t] = tile_product(y, t)
         return 0
 
-    if DIRECT:
-        for j in range(2):
-            w_move(LINE + core, j, mate, 7, chip_rows(core)).wait_recv()
-            cp = w_move(LINE + core, j, mate, 7, chip_rows(core))
-            cp.start()
-            sends.append(cp)
     for j in range(2):
         h = behind * 2 + core
         w_move(h, j, mate, 0).wait_recv()
@@ -607,8 +601,14 @@
         h = ahead * 2 + core
         w_move(h, j, mate, 0).wait_recv()
         w_send(h, j, mate, 5)
+    if DIRECT:
+        for j in range(2):
+            w_move(LINE + core, j, mate, 7, chip_rows(core)).wait_recv()
+            cp = w_move(LINE + core, j, mate, 7, chip_rows(core))
+            cp.start()
+            sends.append(cp)
+    lax.fori_loop(0, tiles, second, 0)
     lax.fori_loop(0, tiles, own_tile, 0)
-    lax.fori_loop(0, tiles, second, 0)
     for j in range(2):
         h = ((x + 2) % CHIPS) * 2 + core
         w_move(h, j, mate, 0).wait_recv()

time: 60.2 us -> 60.2 us (level)
  no operation moved by 1% of the time
where the time goes in v6:
time: 60.2 us; the launch traced here: 60.1 us
  Pallas kernels  59.1 us (98%)
  local copies, waits for them, and re-layouts  0.97 us (2%)
    pallas_call x1, Pallas kernels, local(): pl.pallas_call(kernel, out_shape=pltpu.VMEM((tok, width), BF), in_specs=[...  59.1 us

profile of v6, /device:TPU:1, one launch (start us, length us, event | category | flops | bytes accessed | tf_op | source)
XLA Modules:
  0.0 60.1 jit_solution(3711480989956598496)
XLA Ops:
  0.0 59.1 %shard_map.55 = bf16[512,1024]{1,0:T(8,128)(2,1)S(1)} custom-call(bf16[512,1024]{1,0:T(8,128)(2,1)} %q_hbm.1, bf16[512,1024]{1,0:T(8,128)(2,1)} %k_hbm.1, bf16[512,1024]{1,0:T(8,128)(2,1)} %v_hbm.1, f32[9,8,512]{2,1,0:T(8,128)} %bitcast.1, bf16[1024,4096]{1,0:T(8,128)(2,1)} %w_hbm.1), custom_call_target="tpu_custom_call" | custom-call | tf_op jit(solution)/shard_map/pallas_call | solution.py:804
  59.1 1.0 %copy.7 = bf16[512,1024]{1,0:T(8,128)(2,1)} copy(bf16[512,1024]{1,0:T(8,128)(2,1)S(1)} %shard_map.55) | data formatting | bytes 2097152
